TPU v7x, 256 devices: a whole 4x4x8 slice. The times are simulated.
256 devices in a mesh: fact: 64 (over z, y, core), feat: 4 (over x).
Axes of the slice: x: 4, y: 4, z: 8, core: 2. Of those that a mesh axis runs over, the one named last changes fastest.
Arguments:
- fact_x: bfloat16 [65536, 512], P('fact', 'feat'), may hold values from -16 to 16
- dim_owner: int32 [65536, 1], P('fact'), may hold values from 0 to 63; in each aligned block of 1024 rows (0 to 1023, 1024 to 2047, ...) at most 48 rows name the same one
- dim_slot: int32 [65536], P('fact'), may hold values from 0 to 127
- fact_owner: int32 [65536, 1], P('fact'), may hold values from 0 to 63; in each aligned block of 1024 rows (0 to 1023, 1024 to 2047, ...) at most 48 rows name the same one
- fact_slot: int32 [65536], P('fact'), may hold values from 0 to 127
- dim_table: bfloat16 [8192, 512], P('fact', 'feat'), may hold values from -6 to 6
- entity_h: bfloat16 [8192, 512], P('fact', 'feat'), may hold values from -16 to 16
- w_msg: bfloat16 [512, 512], P(None, 'feat'), may hold values from -0.25 to 0.25
- w_self: bfloat16 [512, 512], P(None, 'feat'), may hold values from -0.25 to 0.25
- w_neigh: bfloat16 [512, 512], P(None, 'feat'), may hold values from -0.25 to 0.25
- cotangent: bfloat16 [8192, 512], P('fact', 'feat'), may hold values from -0.59765625 to 0.59765625
Outputs:
- output_h: bfloat16 [8192, 512], P('fact', 'feat')
- grad_w_msg: float32 [512, 512], P('fact', 'feat')
- grad_w_self: float32 [512, 512], P('fact', 'feat')
- grad_w_neigh: float32 [512, 512], P('fact', 'feat')
- grad_dim: float32 [8192, 512], P('fact', 'feat')
Inputs may be any that keep to these rules, and one draw needn't show every extreme that they name: `fact_owner`: among the fact rows of one index of fact, no key range is named by more than 48 rows, and some key range by exactly 48. `dim_owner`: among the fact rows of one index of fact, no block of the dimension table is named by more than 48 rows, and some block by exactly 48.
All inputs are finite; a program needn't handle non-finite values.
Results may differ from a plain program's by a relative error of at most 0.0059.
Values may be sent and summed in bfloat16 or wider, within the bound.
A program may use at most 64 MiB of HBM per device.

v0:
```python
import math
import jax
import jax.numpy as jnp
from jax import lax
from jax.sharding import PartitionSpec as P


def silu_slope(values):
    sigmoid_v = jax.nn.sigmoid(values)
    return sigmoid_v * (1.0 + values * (1.0 - sigmoid_v))


def pick_rows(row_keys, table):
    table_rows = table.shape[0]
    block_len = math.gcd(table_rows, 1024)
    num_blocks = table_rows // block_len
    blocks = table.reshape(num_blocks, block_len, table.shape[1])
    columns = lax.iota(jnp.int32, block_len)

    def advance(running, block_no):
        block = lax.dynamic_index_in_dim(blocks, block_no, 0, keepdims=False)
        selector = (row_keys[:, None] == block_no * block_len + columns[None, :]).astype(
            jnp.bfloat16
        )
        return (running + jnp.dot(selector, block, preferred_element_type=jnp.float32), None)

    initial = jnp.zeros((row_keys.shape[0], table.shape[1]), jnp.float32)
    running, _ = lax.scan(advance, initial, jnp.arange(num_blocks, dtype=jnp.int32))
    return running


def sum_rows(row_keys, values, extent):
    block_len = math.gcd(extent, 1024)
    num_blocks = extent // block_len
    targets = lax.iota(jnp.int32, block_len)

    def column_block(block_no):
        selector = (row_keys[None, :] - block_no * block_len == targets[:, None]).astype(
            jnp.bfloat16
        )
        return jnp.dot(selector, values, preferred_element_type=jnp.float32)

    stacked = lax.map(column_block, jnp.arange(num_blocks, dtype=jnp.int32))
    return stacked.reshape(extent, values.shape[1])


def shards(
    fact_x,
    dim_owner,
    dim_slot,
    fact_owner,
    fact_slot,
    dim_table,
    entity_h,
    w_msg,
    w_self,
    w_neigh,
    cotangent,
):
    ent_rows = entity_h.shape[0]
    dim_local = dim_table.shape[0]
    owners = lax.axis_size("fact")
    owner_ids = fact_owner[:, 0]
    entity = owner_ids * ent_rows + fact_slot
    dim_blocks = dim_owner[:, 0]
    fact_dim = dim_blocks * dim_local + dim_slot
    x_full = lax.all_gather(fact_x, "feat", axis=1, tiled=True)
    looked = pick_rows(fact_dim, lax.all_gather(dim_table, "fact", axis=0, tiled=True))
    msg_pre = jnp.dot(x_full, w_msg, preferred_element_type=jnp.float32) + looked
    message = jax.nn.silu(msg_pre).astype(jnp.bfloat16)
    entity_sums = lax.psum_scatter(
        sum_rows(entity, message, ent_rows * lax.axis_size("fact")),
        "fact",
        scatter_dimension=0,
        tiled=True,
    )
    hits = jnp.zeros((ent_rows * owners,), jnp.float32).at[entity].add(1.0)
    counts = lax.psum_scatter(hits, "fact", scatter_dimension=0, tiled=True)
    divisor = jnp.maximum(counts, 1.0)
    aggregate = (entity_sums / divisor[:, None]).astype(jnp.bfloat16)
    h_full, agg_full = (
        lax.all_gather(entity_h, "feat", axis=1, tiled=True),
        lax.all_gather(aggregate, "feat", axis=1, tiled=True),
    )
    pre_act = jnp.dot(h_full, w_self, preferred_element_type=jnp.float32) + jnp.dot(
        agg_full, w_neigh, preferred_element_type=jnp.float32
    )
    output_h = jax.nn.silu(pre_act).astype(jnp.bfloat16)
    d_pre = (cotangent.astype(jnp.float32) * silu_slope(pre_act)).astype(jnp.bfloat16)
    agg_term = jnp.einsum("ej,aj->ea", d_pre, w_neigh, preferred_element_type=jnp.float32)
    d_agg = lax.psum_scatter(agg_term, "feat", scatter_dimension=1, tiled=True)
    d_scaled = (d_agg / divisor[:, None]).astype(jnp.bfloat16)
    d_message = pick_rows(entity, lax.all_gather(d_scaled, "fact", axis=0, tiled=True)).astype(
        jnp.bfloat16
    )
    d_msgpre = (d_message.astype(jnp.float32) * silu_slope(msg_pre)).astype(jnp.bfloat16)
    grad_dim = lax.psum_scatter(
        sum_rows(fact_dim, d_msgpre, dim_local * lax.axis_size("fact")),
        "fact",
        scatter_dimension=0,
        tiled=True,
    )
    self_part = jnp.einsum("ea,eb->ab", h_full, d_pre, preferred_element_type=jnp.float32)
    neigh_part = jnp.einsum("ea,eb->ab", agg_full, d_pre, preferred_element_type=jnp.float32)
    msg_part = jnp.einsum("fa,fb->ab", x_full, d_msgpre, preferred_element_type=jnp.float32)
    grad_w_self, grad_w_neigh, grad_w_msg = (
        lax.psum_scatter(self_part, "fact", scatter_dimension=0, tiled=True),
        lax.psum_scatter(neigh_part, "fact", scatter_dimension=0, tiled=True),
        lax.psum_scatter(msg_part, "fact", scatter_dimension=0, tiled=True),
    )
    return (output_h, grad_w_msg, grad_w_self, grad_w_neigh, grad_dim)


def solution(mesh):
    placed = (
        P("fact", "feat"),
        P("fact", None),
        P("fact"),
        P("fact", None),
        P("fact"),
        P("fact", "feat"),
        P("fact", "feat"),
        P(None, "feat"),
        P(None, "feat"),
        P(None, "feat"),
        P("fact", "feat"),
    )
    return jax.shard_map(
        shards,
        mesh=mesh,
        in_specs=placed,
        out_specs=(
            P("fact", "feat"),
            P("fact", "feat"),
            P("fact", "feat"),
            P("fact", "feat"),
            P("fact", "feat"),
        ),
        check_vma=False,
    )
```

profile of v0, /device:TPU:2, one launch (start us, length us, event | category | flops | bytes accessed | tf_op | source)
XLA Modules:
  0.0 919.5 jit_solution(5410309900059285577)
XLA Ops:
  11.5 79.6 %all-gather.6.cloned.1.call-done = bf16[8192,128]{1,0:T(8,128)(2,1)} async-done(((bf16[128,128]{1,0:T(8,128)(2,1)}), bf16[8192,128]{1,0:T(8,128)(2,1)}) %all-gather.6.cloned.1.call-update) | async-done | bytes 2097168 | tf_op jit(solution)/shard_map/all_gather | solution.py:68
  91.1 40.7 %while.46 = (s32[]{:T(128)}, f32[1024,128]{1,0:T(8,128)S(1)}, s32[1024]{0:T(1024)S(1)}, s32[8]{0:T(128)S(1)}, bf16[8,1024,128]{2,1,0:T(8,128)(2,1)}, /*index=5*/s32[]{:T(128)}, s32[]{:T(128)}, s32[]{:T(128)}, s32[]{:T(128)}) while((s32[]{:T(128)}, f32[1024,128]{1,0:T(8,128)S(1)}, s32[1024]{0:T(1024)S(1)}, s32[8]{0:T(128)S(1)}, ...), condition=%wide.region_1.2_spmd.clone, body=%wide.region_0.1_spmd.clone.sunk | while | flops 269747200 | bytes 1323177 | solution.py:28
  94.3 1.9 fusion.73
  99.3 1.9 fusion.73
  104.4 1.9 fusion.73
  109.5 1.9 fusion.73
  114.6 1.9 fusion.73
  119.7 1.9 fusion.73
  124.8 1.9 fusion.73
  129.9 1.9 fusion.73
  131.8 1.7 multiply_convert_fusion.1
  133.5 2.3 broadcast.43.clone
  135.8 22.6 %while.44 = (s32[]{:T(128)}, f32[8,1024,128]{2,1,0:T(8,128)}, s32[8]{0:T(128)S(1)}, s32[1024]{0:T(1024)S(1)}, bf16[1024,128]{1,0:T(8,128)(2,1)S(1)}, /*index=5*/s32[]{:T(128)}, s32[1]{0:T(128)}) while((s32[]{:T(128)}, f32[8,1024,128]{2,1,0:T(8,128)}, s32[8]{0:T(128)S(1)}, s32[1024]{0:T(1024)S(1)}, bf16[1024,128]{1,0:T(8,128)(2,1)S(1)}, ...), condition=%wide.region_3.4_spmd.clone, body=%wide.region_2.3_spmd.clone.sunk | while | flops 269485056 | bytes 799337 | solution.py:43
  160.4 5.9 scatter_custom_fusion
  166.3 248.9 %all-reduce = f32[8192]{0:T(1024)S(1)} all-reduce(f32[8192]{0:T(1024)S(1)} %scatter_custom_fusion), channel_id=3, replica_groups=mesh['fact'=64,'feat'=4] {'fact'}, use_global_device_ids=true, to_apply=%region_6.7.clone | all-reduce | flops 8192 | bytes 65536
  415.2 11.3 %all_gather.15 = bf16[128,512]{1,0:T(8,128)(2,1)S(1)} all-gather(bf16[128,128]{1,0:T(8,128)(2,1)S(1)} %copy-done.4), channel_id=1, replica_groups=mesh['fact'=64,'feat'=4] {'feat'}, dimensions={1}, use_global_device_ids=true | all-gather | bytes 163840 | tf_op jit(solution)/shard_map/all_gather | solution.py:82
  427.7 10.4 %all_gather.18 = bf16[128,512]{1,0:T(8,128)(2,1)S(1)} all-gather(bf16[128,128]{1,0:T(8,128)(2,1)S(1)} %divide_convert_fusion.1), channel_id=1, replica_groups=mesh['fact'=64,'feat'=4] {'feat'}, dimensions={1}, use_global_device_ids=true | all-gather | bytes 163840 | tf_op jit(solution)/shard_map/all_gather | solution.py:83
  439.9 18.9 %reduce-scatter.8.cloned.1.call-done = f32[128,128]{1,0:T(8,128)} async-done(((f32[128,512]{1,0:T(8,128)}), f32[128,128]{1,0:T(8,128)}) %reduce-scatter.8.cloned.1.call-update) | async-done | bytes 65552 | tf_op jit(solution)/shard_map/reduce_scatter | solution.py:91
  462.3 78.6 %all-gather.8.cloned.1.call-done = bf16[8192,128]{1,0:T(8,128)(2,1)} async-done(((bf16[128,128]{1,0:T(8,128)(2,1)}), bf16[8192,128]{1,0:T(8,128)(2,1)}) %all-gather.8.cloned.1.call-update) | async-done | bytes 2097168 | tf_op jit(solution)/shard_map/all_gather | solution.py:93
  540.9 40.7 %while.47 = (s32[]{:T(128)}, f32[1024,128]{1,0:T(8,128)S(1)}, s32[1024]{0:T(1024)S(1)}, s32[8]{0:T(128)S(1)}, bf16[8,1024,128]{2,1,0:T(8,128)(2,1)}, /*index=5*/s32[]{:T(128)}, s32[]{:T(128)}, s32[]{:T(128)}, s32[]{:T(128)}) while((s32[]{:T(128)}, f32[1024,128]{1,0:T(8,128)S(1)}, s32[1024]{0:T(1024)S(1)}, s32[8]{0:T(128)S(1)}, ...), condition=%wide.region_9.10_spmd.clone, body=%wide.region_8.9_spmd.clone.sunk | while | flops 269747200 | bytes 1323177 | solution.py:28
  544.1 1.9 fusion.76
  549.2 1.9 fusion.76
  554.3 1.9 fusion.76
  559.4 1.9 fusion.76
  564.5 1.9 fusion.76
  569.5 1.9 fusion.76
  574.6 1.9 fusion.76
  579.7 1.9 fusion.76
  583.0 2.3 broadcast.43
  585.2 22.6 %while.45 = (s32[]{:T(128)}, f32[8,1024,128]{2,1,0:T(8,128)}, s32[8]{0:T(128)S(1)}, s32[1024]{0:T(1024)S(1)}, bf16[1024,128]{1,0:T(8,128)(2,1)S(1)}, /*index=5*/s32[]{:T(128)}, s32[1]{0:T(128)}) while((s32[]{:T(128)}, f32[8,1024,128]{2,1,0:T(8,128)}, s32[8]{0:T(128)S(1)}, s32[1024]{0:T(1024)S(1)}, ...), condition=%wide.region_14.15_spmd.clone, body=%wide.region_13.14_spmd.clone.sunk | while | flops 269485056 | bytes 799337 | solution.py:43
  608.6 156.2 %all-reduce.7.cloned.1.call-done = (f32[512,128]{0,1:T(8,128)}, f32[512,128]{0,1:T(8,128)}, f32[512,128]{1,0:T(8,128)}) async-done(((f32[512,128]{0,1:T(8,128)}, f32[512,128]{0,1:T(8,128)}, f32[512,128]{1,0:T(8,128)}), (f32[512,128]{0,1:T(8,128)}, f32[512,128]{0,1:T(8,128)}, f32[512,128]{1,0:T(8,128)})) %all-reduce.7.cloned.1.call-update) | async-done | bytes 786448
  768.3 144.4 %reduce-scatter.10.cloned.1.call-done = f32[128,128]{1,0:T(8,128)} async-done(((f32[8192,128]{1,0:T(8,128)}), f32[128,128]{1,0:T(8,128)}) %reduce-scatter.10.cloned.1.call-update) | async-done | bytes 65552 | tf_op jit(solution)/shard_map/reduce_scatter | solution.py:97
  (136 shorter events, 60.9 us)
Async XLA Ops:
  7.2 124.6 %copy-start = (bf16[512,128]{1,0:T(8,128)(2,1)S(1)}, bf16[512,128]{1,0:T(8,128)(2,1)}, u32[]{:S(2)}) copy-start(bf16[512,128]{1,0:T(8,128)(2,1)} %param.26) | copy-start | bytes 393220
  7.2 83.9 %all-gather.6.cloned.1.call-start = ((), (), s32[]{:S(2)}) async-start(), calls=%async_computation.4 | async-start | bytes 2129920 | tf_op jit(solution)/shard_map/all_gather | solution.py:68
  7.9 123.9 %all-gather.4.cloned.1.call-start = ((), (), s32[]{:S(2)}) async-start(), calls=%async_computation.3 | async-start | bytes 1310720 | tf_op jit(solution)/shard_map/all_gather | solution.py:67
  8.7 418.1 %reduce-scatter.6.cloned.1.call-start = ((), (), s32[]{:S(2)}) async-start(), calls=%async_computation.5 | async-start | bytes 4259840 | tf_op jit(solution)/shard_map/reduce_scatter | solution.py:71
  158.4 0.7 copy-start.6
  158.4 256.8 %copy-start.4 = (bf16[128,128]{1,0:T(8,128)(2,1)S(1)}, bf16[128,128]{1,0:T(8,128)(2,1)}, u32[]{:S(2)}) copy-start(bf16[128,128]{1,0:T(8,128)(2,1)} %param.25) | copy-start | bytes 98308
  158.4 268.1 %copy-start.2 = (bf16[512,128]{1,0:T(8,128)(2,1)S(1)}, bf16[512,128]{1,0:T(8,128)(2,1)}, u32[]{:S(2)}) copy-start(bf16[512,128]{1,0:T(8,128)(2,1)} %param.27) | copy-start | bytes 393220
  158.4 279.7 %copy-start.3 = (bf16[512,128]{1,0:T(8,128)(2,1)S(1)}, bf16[512,128]{1,0:T(8,128)(2,1)}, u32[]{:S(2)}) copy-start(bf16[512,128]{1,0:T(8,128)(2,1)} %param.28) | copy-start | bytes 393220
  158.5 279.7 %copy-start.5 = (bf16[128,128]{1,0:T(8,128)(2,1)S(1)}, bf16[128,128]{1,0:T(8,128)(2,1)}, u32[]{:S(2)}) copy-start(bf16[128,128]{1,0:T(8,128)(2,1)} %param.29) | copy-start | bytes 98308
  158.5 300.4 %reduce-scatter.8.cloned.1.call-start = ((), (), s32[]{:S(2)}) async-start(), calls=%async_computation.6 | async-start | bytes 327680 | tf_op jit(solution)/shard_map/reduce_scatter | solution.py:91
  439.9 101.0 %all-gather.8.cloned.1.call-start = ((), (), s32[]{:S(2)}) async-start(), calls=%async_computation.7 | async-start | bytes 2129920 | tf_op jit(solution)/shard_map/all_gather | solution.py:93
  460.4 304.3 %all-reduce.7.cloned.1.call-start = ((), (), s32[]{:S(2)}) async-start(), calls=%async_computation.9 | async-start | bytes 1572864
  540.9 40.9 %copy-start.1 = (bf16[1024,512]{1,0:T(8,128)(2,1)S(1)}, bf16[1024,512]{1,0:T(8,128)(2,1)}, u32[]{:S(2)}) copy-start(bf16[1024,512]{1,0:T(8,128)(2,1)} %all-gather.4.cloned.1.call-done) | copy-start | bytes 3145732
  582.9 329.8 %reduce-scatter.10.cloned.1.call-start = ((), (), s32[]{:S(2)}) async-start(), calls=%async_computation.8 | async-start | bytes 4259840 | tf_op jit(solution)/shard_map/reduce_scatter | solution.py:97
Sparse Core Ops, SparseCore 0:
  10.8 80.2 all-gather.5
  92.9 25.4 all-gather.3
  158.6 141.5 reduce-scatter.5
  440.0 18.7 reduce-scatter.7
  462.0 78.8 all-gather.7
  583.0 181.6 all-reduce.6
  770.0 142.6 reduce-scatter.9
where the time goes:
time: 921 us; the launch traced here: 920 us
  waiting for transfers between devices  479 us (52%)
  blocking collectives  271 us (29%)
  matrix products  61.8 us (7%)
  loops' own time  52.5 us (6%)
  local copies, waits for them, and re-layouts  28 us (3%)
  between operations  15.6 us (2%)
  other arithmetic  11.6 us (1%)
    unnamed x1, blocking collectives  249 us
    unnamed x8, waiting for transfers between devices  158 us
    reduce_scatter x1, waiting for transfers between devices, shards(): lax.psum_scatter(sum_rows(fact_dim, d_msgpre, dim_local * lax.axis_size('...  144 us
    all_gather x1, waiting for transfers between devices, shards(): lax.all_gather(dim_table, 'fact', axis=0, tiled=True)  79.6 us
    all_gather x1, waiting for transfers between devices, shards(): lax.all_gather(d_scaled, 'fact', axis=0, tiled=True)  78.6 us
    another operation x2, loops' own time, pick_rows(): lax.scan(advance, initial, jnp.arange(num_blocks, dtype=jnp.int32))  42 us
    dot_general x16, matrix products, advance(): jnp.dot(selector, block, preferred_element_type=jnp.float32)  30 us
    dot_general x16, matrix products, column_block(): return jnp.dot(selector, values, preferred_element_type=jnp.float32)  25.3 us
  transfers between devices with their start and end apart: 7, of which 5 were waited for; matrix products, arithmetic and copies ran while one was open for 6% of the time, Pallas kernels for 0%

commit v1 on v0

--- a/solution.py
+++ b/solution.py
@@ -1,8 +1,18 @@
+import functools
 import math
 import jax
 import jax.numpy as jnp
 from jax import lax
 from jax.sharding import PartitionSpec as P
+
+
+def fit_the_racks(field_in, link_axis, ndim_at):
+    all_values = jnp.stack([field_in for _ in range(lax.psum(1, link_axis))])
+    reached = lax.all_to_all(all_values, link_axis, 0, 0)
+    return jnp.concatenate(reached, axis=ndim_at)
+
+
+hold_face = functools.partial(fit_the_racks, link_axis="fact", ndim_at=0)
 
 
 def silu_slope(values):
@@ -90,9 +100,7 @@
     agg_term = jnp.einsum("ej,aj->ea", d_pre, w_neigh, preferred_element_type=jnp.float32)
     d_agg = lax.psum_scatter(agg_term, "feat", scatter_dimension=1, tiled=True)
     d_scaled = (d_agg / divisor[:, None]).astype(jnp.bfloat16)
-    d_message = pick_rows(entity, lax.all_gather(d_scaled, "fact", axis=0, tiled=True)).astype(
-        jnp.bfloat16
-    )
+    d_message = pick_rows(entity, hold_face(d_scaled)).astype(jnp.bfloat16)
     d_msgpre = (d_message.astype(jnp.float32) * silu_slope(msg_pre)).astype(jnp.bfloat16)
     grad_dim = lax.psum_scatter(
         sum_rows(fact_dim, d_msgpre, dim_local * lax.axis_size("fact")),

time: 921 us -> 910 us (0.988)
  waiting for transfers between devices: 479 us -> 449 us
  starting transfers between devices: 0.28 us -> 10.7 us
    all_gather x1 -> x0, waiting for transfers between devices: 78.6 us -> none  [shards(): lax.all_gather(d_scaled, 'fact', axis=0, tiled=True)]
    all_to_all x0 -> x1, waiting for transfers between devices: none -> 49.5 us  [fit_the_racks(): reached = lax.all_to_all(all_values, link_axis, 0, 0)]
    all_to_all x0 -> x1, starting transfers between devices: none -> 10.5 us  [fit_the_racks(): reached = lax.all_to_all(all_values, link_axis, 0, 0)]
    unnamed x8 -> x7, waiting for transfers between devices: 158 us -> 156 us
where the time goes in v1:
time: 910 us; the launch traced here: 908 us
  waiting for transfers between devices  449 us (49%)
  blocking collectives  271 us (30%)
  matrix products  67.9 us (7%)
  loops' own time  52.4 us (6%)
  local copies, waits for them, and re-layouts  29.9 us (3%)
  between operations  15.6 us (2%)
  other arithmetic  12.2 us (1%)
  starting transfers between devices  10.7 us (1%)
    unnamed x1, blocking collectives  249 us
    unnamed x7, waiting for transfers between devices  156 us
    reduce_scatter x1, waiting for transfers between devices, shards(): lax.psum_scatter(sum_rows(fact_dim, d_msgpre, dim_local * lax.axis_size('...  144 us
    all_gather x1, waiting for transfers between devices, shards(): lax.all_gather(dim_table, 'fact', axis=0, tiled=True)  79.6 us
    all_to_all x1, waiting for transfers between devices, fit_the_racks(): reached = lax.all_to_all(all_values, link_axis, 0, 0)  49.5 us
    another operation x2, loops' own time, pick_rows(): lax.scan(advance, initial, jnp.arange(num_blocks, dtype=jnp.int32))  41.8 us
    dot_general x16, matrix products, advance(): jnp.dot(selector, block, preferred_element_type=jnp.float32)  35.3 us
    dot_general x16, matrix products, column_block(): return jnp.dot(selector, values, preferred_element_type=jnp.float32)  25.4 us
  transfers between devices with their start and end apart: 7, of which 5 were waited for; matrix products, arithmetic and copies ran while one was open for 6% of the time, Pallas kernels for 0%

profile of v1, /device:TPU:2, one launch (start us, length us, event | category | flops | bytes accessed | tf_op | source)
XLA Modules:
  0.0 907.8 jit_solution(1403976932214309614)
XLA Ops:
  11.5 79.6 %all-gather.5.cloned.1.call-done = bf16[8192,128]{1,0:T(8,128)(2,1)} async-done(((bf16[128,128]{1,0:T(8,128)(2,1)}), bf16[8192,128]{1,0:T(8,128)(2,1)}) %all-gather.5.cloned.1.call-update) | async-done | bytes 2097168 | tf_op jit(solution)/shard_map/all_gather | solution.py:78
  91.1 40.7 %while.46 = (s32[]{:T(128)}, f32[1024,128]{1,0:T(8,128)S(1)}, s32[1024]{0:T(1024)S(1)}, s32[8]{0:T(128)S(1)}, bf16[8,1024,128]{2,1,0:T(8,128)(2,1)}, /*index=5*/s32[]{:T(128)}, s32[]{:T(128)}, s32[]{:T(128)}, s32[]{:T(128)}) while((s32[]{:T(128)}, f32[1024,128]{1,0:T(8,128)S(1)}, s32[1024]{0:T(1024)S(1)}, s32[8]{0:T(128)S(1)}, ...), condition=%wide.region_1.2_spmd.clone, body=%wide.region_0.1_spmd.clone.sunk | while | flops 269747200 | bytes 1323177 | solution.py:38
  94.3 1.9 fusion.73
  99.3 1.9 fusion.73
  104.4 1.9 fusion.73
  109.5 1.9 fusion.73
  114.6 1.9 fusion.73
  119.7 1.9 fusion.73
  124.8 1.9 fusion.73
  129.9 1.9 fusion.73
  131.8 2.5 multiply_convert_fusion.1
  134.3 2.3 broadcast.45.clone
  136.6 22.7 %while.44 = (s32[]{:T(128)}, f32[8,1024,128]{2,1,0:T(8,128)}, s32[8]{0:T(128)S(1)}, s32[1024]{0:T(1024)S(1)}, bf16[1024,128]{1,0:T(8,128)(2,1)S(1)}, /*index=5*/s32[]{:T(128)}, s32[1]{0:T(128)}) while((s32[]{:T(128)}, f32[8,1024,128]{2,1,0:T(8,128)}, s32[8]{0:T(128)S(1)}, s32[1024]{0:T(1024)S(1)}, bf16[1024,128]{1,0:T(8,128)(2,1)S(1)}, ...), condition=%wide.region_3.4_spmd.clone, body=%wide.region_2.3_spmd.clone.sunk | while | flops 269485056 | bytes 799337 | solution.py:53
  161.2 5.9 scatter_custom_fusion
  167.2 248.8 %all-reduce = f32[8192]{0:T(1024)S(1)} all-reduce(f32[8192]{0:T(1024)S(1)} %scatter_custom_fusion), channel_id=3, replica_groups=mesh['fact'=64,'feat'=4] {'fact'}, use_global_device_ids=true, to_apply=%region_6.7.clone | all-reduce | flops 8192 | bytes 65536
  416.0 11.4 %all_gather.12 = bf16[128,512]{1,0:T(8,128)(2,1)S(1)} all-gather(bf16[128,128]{1,0:T(8,128)(2,1)S(1)} %copy-done.4), channel_id=1, replica_groups=mesh['fact'=64,'feat'=4] {'feat'}, dimensions={1}, use_global_device_ids=true | all-gather | bytes 163840 | tf_op jit(solution)/shard_map/all_gather | solution.py:92
  428.6 10.4 %all_gather.15 = bf16[128,512]{1,0:T(8,128)(2,1)S(1)} all-gather(bf16[128,128]{1,0:T(8,128)(2,1)S(1)} %divide_convert_fusion.1), channel_id=1, replica_groups=mesh['fact'=64,'feat'=4] {'feat'}, dimensions={1}, use_global_device_ids=true | all-gather | bytes 163840 | tf_op jit(solution)/shard_map/all_gather | solution.py:93
  440.7 18.9 %reduce-scatter.8.cloned.1.call-done = f32[128,128]{1,0:T(8,128)} async-done(((f32[128,512]{1,0:T(8,128)}), f32[128,128]{1,0:T(8,128)}) %reduce-scatter.8.cloned.1.call-update) | async-done | bytes 65552 | tf_op jit(solution)/shard_map/reduce_scatter | solution.py:101
  462.4 10.5 %all-to-all-start = ((bf16[64,128,128]{2,1,0:T(8,128)(2,1)}), bf16[64,128,128]{2,1,0:T(8,128)(2,1)S(1)}, u32[]{:S(2)}, u32[]{:S(2)}) async-start(bf16[64,128,128]{2,1,0:T(8,128)(2,1)} %stack.2), calls=%async_computation.2 | async-start | bytes 4194304 | tf_op jit(solution)/shard_map/all_to_all | solution.py:11
  474.8 49.5 %all-to-all-done = bf16[64,128,128]{2,1,0:T(8,128)(2,1)S(1)} async-done(((bf16[64,128,128]{2,1,0:T(8,128)(2,1)}), bf16[64,128,128]{2,1,0:T(8,128)(2,1)S(1)}, u32[]{:S(2)}, u32[]{:S(2)}) %all-to-all-start) | async-done | bytes 2097184 | tf_op jit(solution)/shard_map/all_to_all | solution.py:11
  524.2 45.8 %while.47 = (s32[]{:T(128)}, f32[1024,128]{1,0:T(8,128)}, s32[1024]{0:T(1024)S(1)}, s32[8]{0:T(128)S(1)}, bf16[8,1024,128]{2,1,0:T(8,128)(2,1)S(1)}, /*index=5*/s32[]{:T(128)}, s32[]{:T(128)}, s32[]{:T(128)}, s32[]{:T(128)}) while((s32[]{:T(128)}, f32[1024,128]{1,0:T(8,128)}, s32[1024]{0:T(1024)S(1)}, s32[8]{0:T(128)S(1)}, ...), condition=%wide.region_9.10_spmd.clone, body=%wide.region_8.9_spmd.clone.sunk | while | flops 269747200 | bytes 1323177 | solution.py:38
  532.2 2.7 fusion.76
  538.1 2.7 fusion.76
  543.9 2.7 fusion.76
  549.8 2.7 fusion.76
  555.6 2.7 fusion.76
  561.5 2.7 fusion.76
  567.4 2.7 fusion.76
  572.5 2.3 broadcast.45
  574.8 22.7 %while.45 = (s32[]{:T(128)}, f32[8,1024,128]{2,1,0:T(8,128)}, s32[8]{0:T(128)S(1)}, s32[1024]{0:T(1024)S(1)}, bf16[1024,128]{1,0:T(8,128)(2,1)S(1)}, /*index=5*/s32[]{:T(128)}, s32[1]{0:T(128)}) while((s32[]{:T(128)}, f32[8,1024,128]{2,1,0:T(8,128)}, s32[8]{0:T(128)S(1)}, s32[1024]{0:T(1024)S(1)}, ...), condition=%wide.region_14.15_spmd.clone, body=%wide.region_13.14_spmd.clone.sunk | while | flops 269485056 | bytes 799337 | solution.py:53
  598.2 155.0 %all-reduce.7.cloned.1.call-done = (f32[512,128]{0,1:T(8,128)}, f32[512,128]{0,1:T(8,128)}, f32[512,128]{1,0:T(8,128)}) async-done(((f32[512,128]{0,1:T(8,128)}, f32[512,128]{0,1:T(8,128)}, f32[512,128]{1,0:T(8,128)}), (f32[512,128]{0,1:T(8,128)}, f32[512,128]{0,1:T(8,128)}, f32[512,128]{1,0:T(8,128)})) %all-reduce.7.cloned.1.call-update) | async-done | bytes 786448
  756.7 144.2 %reduce-scatter.10.cloned.1.call-done = f32[128,128]{1,0:T(8,128)} async-done(((f32[8192,128]{1,0:T(8,128)}), f32[128,128]{1,0:T(8,128)}) %reduce-scatter.10.cloned.1.call-update) | async-done | bytes 65552 | tf_op jit(solution)/shard_map/reduce_scatter | solution.py:105
  (136 shorter events, 64.9 us)
Async XLA Ops:
  7.2 124.6 %copy-start = (bf16[512,128]{1,0:T(8,128)(2,1)S(1)}, bf16[512,128]{1,0:T(8,128)(2,1)}, u32[]{:S(2)}) copy-start(bf16[512,128]{1,0:T(8,128)(2,1)} %param.26) | copy-start | bytes 393220
  7.2 83.9 %all-gather.5.cloned.1.call-start = ((), (), s32[]{:S(2)}) async-start(), calls=%async_computation.5 | async-start | bytes 2129920 | tf_op jit(solution)/shard_map/all_gather | solution.py:78
  7.9 123.9 %all-gather.3.cloned.1.call-start = ((), (), s32[]{:S(2)}) async-start(), calls=%async_computation.4 | async-start | bytes 1310720 | tf_op jit(solution)/shard_map/all_gather | solution.py:77
  8.7 419.0 %reduce-scatter.6.cloned.1.call-start = ((), (), s32[]{:S(2)}) async-start(), calls=%async_computation.6 | async-start | bytes 4259840 | tf_op jit(solution)/shard_map/reduce_scatter | solution.py:81
  159.3 0.7 copy-start.6
  159.3 256.7 %copy-start.4 = (bf16[128,128]{1,0:T(8,128)(2,1)S(1)}, bf16[128,128]{1,0:T(8,128)(2,1)}, u32[]{:S(2)}) copy-start(bf16[128,128]{1,0:T(8,128)(2,1)} %param.25) | copy-start | bytes 98308
  159.3 268.1 %copy-start.2 = (bf16[512,128]{1,0:T(8,128)(2,1)S(1)}, bf16[512,128]{1,0:T(8,128)(2,1)}, u32[]{:S(2)}) copy-start(bf16[512,128]{1,0:T(8,128)(2,1)} %param.27) | copy-start | bytes 393220
  159.3 279.7 %copy-start.3 = (bf16[512,128]{1,0:T(8,128)(2,1)S(1)}, bf16[512,128]{1,0:T(8,128)(2,1)}, u32[]{:S(2)}) copy-start(bf16[512,128]{1,0:T(8,128)(2,1)} %param.28) | copy-start | bytes 393220
  159.3 279.7 %copy-start.5 = (bf16[128,128]{1,0:T(8,128)(2,1)S(1)}, bf16[128,128]{1,0:T(8,128)(2,1)}, u32[]{:S(2)}) copy-start(bf16[128,128]{1,0:T(8,128)(2,1)} %param.29) | copy-start | bytes 98308
  159.3 300.3 %reduce-scatter.8.cloned.1.call-start = ((), (), s32[]{:S(2)}) async-start(), calls=%async_computation.7 | async-start | bytes 327680 | tf_op jit(solution)/shard_map/reduce_scatter | solution.py:101
  462.4 61.8 %all-to-all-start = ((bf16[64,128,128]{2,1,0:T(8,128)(2,1)}), bf16[64,128,128]{2,1,0:T(8,128)(2,1)S(1)}, u32[]{:S(2)}, u32[]{:S(2)}) async-start(bf16[64,128,128]{2,1,0:T(8,128)(2,1)} %stack.2), calls=%async_computation.2 | async-start | bytes 4194304 | tf_op jit(solution)/shard_map/all_to_all | solution.py:11
  472.9 280.3 %all-reduce.7.cloned.1.call-start = ((), (), s32[]{:S(2)}) async-start(), calls=%async_computation.9 | async-start | bytes 1572864
  524.2 47.2 %copy-start.1 = (bf16[1024,512]{1,0:T(8,128)(2,1)S(1)}, bf16[1024,512]{1,0:T(8,128)(2,1)}, u32[]{:S(2)}) copy-start(bf16[1024,512]{1,0:T(8,128)(2,1)} %all-gather.3.cloned.1.call-done) | copy-start | bytes 3145732
  572.5 328.5 %reduce-scatter.10.cloned.1.call-start = ((), (), s32[]{:S(2)}) async-start(), calls=%async_computation.8 | async-start | bytes 4259840 | tf_op jit(solution)/shard_map/reduce_scatter | solution.py:105
Sparse Core Ops, SparseCore 0:
  10.8 80.2 all-gather.4
  92.9 25.4 all-gather.2
  159.4 141.6 reduce-scatter.5
  440.9 18.7 reduce-scatter.7
  572.6 180.5 all-reduce.6
  758.3 142.6 reduce-scatter.9
